TPU v7x, 32 devices: a whole 2x2x4 slice. The times are simulated.
32 devices in a mesh: mode: 16 (over z, x, core), rank: 2 (over y).
Axes of the slice: x: 2, y: 2, z: 4, core: 2. Of those that a mesh axis runs over, the one named last changes fastest.
Arguments:
- core_right: float32 [1024, 256, 1024], P('rank', 'mode'), may hold values from -0.1875 to 0.1875
- sketch_right: float32 [256, 256, 256], P('rank', 'mode'), may hold values from -0.0234375 to 0.0234375
- core_left: float32 [1024, 256, 1024], P('rank', 'mode'), may hold values from -0.1875 to 0.1875
- sketch_left: float32 [256, 256, 256], P('rank', 'mode'), may hold values from -0.0234375 to 0.0234375
- carry_in: float32 [1024, 256], P('rank'), may hold values from -6 to 6
Outputs:
- carry_out: float32 [1024, 256], P('rank')
All inputs are finite; a program needn't handle non-finite values.
Results may differ from a plain program's by a relative error of at most 0.00013.
Values sent between devices are 32-bit elements; how exact they have to be, the bound alone decides.
No kernel may reach another device: no remote copies, remote signals or barrier semaphores. Data moves between devices by JAX's collectives and lax.ppermute only.
A program may use at most 128 MiB of HBM per device.

v0:
```python
import jax
import jax.numpy as jnp
from jax import lax
from jax.sharding import PartitionSpec as P


def chain_step(core, carried, sketch):
    hidden = jnp.einsum("aib,bc->aic", core, carried, precision=lax.Precision.HIGHEST)
    return jnp.einsum("aic,sic->as", hidden, sketch, precision=lax.Precision.HIGHEST)


def shards(core_right, sketch_right, core_left, sketch_left, carry_in):
    sketch_whole_right, sketch_whole_left, carried = (
        lax.all_gather(sketch_right, "rank", axis=0, tiled=True),
        lax.all_gather(sketch_left, "rank", axis=0, tiled=True),
        lax.all_gather(carry_in, "rank", axis=0, tiled=True),
    )
    sketches = (sketch_whole_right, sketch_whole_left)
    cores = (core_right, core_left)
    result = carry_in
    for step in range(2):
        partial_sum = chain_step(cores[step], carried, sketches[step])
        summed = lax.psum(partial_sum, "mode")
        if step == 0:
            carried = lax.all_gather(summed, "rank", axis=0, tiled=True)
        else:
            result = summed
    return result


def solution(mesh):
    in_specs = (
        P("rank", "mode", None),
        P("rank", "mode", None),
        P("rank", "mode", None),
        P("rank", "mode", None),
        P("rank", None),
    )
    out_specs = P("rank", None)
    return jax.shard_map(shards, mesh=mesh, in_specs=in_specs, out_specs=out_specs, check_vma=False)
```

profile of v0, /device:TPU:1, one launch (start us, length us, event | category | flops | bytes accessed | tf_op | source)
XLA Modules:
  0.0 387.6 jit_solution(3806773497062349039)
XLA Ops:
  6.5 0.0 all-gather.5.cloned.1.call-start
  6.5 0.7 all-gather.5.cloned.1.call-update
  7.3 0.0 all-gather.7.cloned.1.call-start
  7.3 0.7 all-gather.7.cloned.1.call-update
  8.0 0.0 all-reduce.3.cloned.1.call-start
  8.1 24.3 %all-gather.5.cloned.1.call-done = f32[1024,256]{1,0:T(8,128)} async-done(((f32[512,256]{1,0:T(8,128)}), f32[1024,256]{1,0:T(8,128)}) %all-gather.5.cloned.1.call-update) | async-done | bytes 1048592 | tf_op jit(solution)/shard_map/all_gather | solution.py:16
  32.3 31.0 %fusion.16 = f32[512,16,256]{2,1,0:T(8,128)} fusion(f32[512,16,1024]{2,1,0:T(8,128)} %param.5, f32[1024,256]{1,0:T(8,128)} %all-gather.5.cloned.1.call-done), kind=kOutput, calls=%fused_computation.10 | convolution fusion | flops 25769803776 | bytes 42991616 | tf_op jit(solution)/shard_map/aib,bc->aic/dot_general | solution.py:8
  63.3 0.0 copy-start
  63.3 27.4 %all-gather.7.cloned.1.call-done = f32[256,16,256]{2,1,0:T(8,128)} async-done(((f32[128,16,256]{2,1,0:T(8,128)}), f32[256,16,256]{2,1,0:T(8,128)}) %all-gather.7.cloned.1.call-update) | async-done | bytes 4194320 | tf_op jit(solution)/shard_map/all_gather | solution.py:14
  90.7 15.1 %fusion.7 = f32[512,256]{1,0:T(8,128)} fusion(f32[256,16,256]{2,1,0:T(8,128)} %all-gather.7.cloned.1.call-done, f32[512,16,256]{2,1,0:T(8,128)} %fusion.16), kind=kOutput, calls=%fused_computation.7 | convolution fusion | flops 6442450944 | bytes 13107200 | tf_op jit(solution)/shard_map/aic,sic->as/dot_general | solution.py:9
  105.8 0.0 all-reduce.3.cloned.1.call-update
  105.8 0.0 all-gather.9.cloned.1.call-start
  105.8 90.8 %all-reduce.3.cloned.1.call-done = f32[512,256]{1,0:T(8,128)} async-done(((f32[512,256]{1,0:T(8,128)}), f32[512,256]{1,0:T(8,128)}) %all-reduce.3.cloned.1.call-update) | async-done | bytes 524304 | tf_op jit(solution)/shard_map/psum | solution.py:23
  196.6 0.0 all-gather.9.cloned.1.call-update
  196.7 0.0 all-gather.11.cloned.1.call-start
  196.7 0.0 copy-done
  196.7 2.5 copy.7
  199.3 0.0 all-gather.11.cloned.1.call-update
  199.3 0.2 all-reduce.5.cloned.1.call-start
  199.5 19.7 %all-gather.9.cloned.1.call-done = f32[1024,256]{1,0:T(8,128)} async-done(((f32[512,256]{1,0:T(8,128)}), f32[1024,256]{1,0:T(8,128)}) %all-gather.9.cloned.1.call-update) | async-done | bytes 1048592 | tf_op jit(solution)/shard_map/all_gather | solution.py:25
  219.3 51.0 %fusion = f32[256,512,16]{0,1,2:T(8,128)} fusion(f32[512,16,1024]{2,1,0:T(8,128)} %param.7, f32[1024,256]{1,0:T(8,128)} %all-gather.9.cloned.1.call-done), kind=kOutput, calls=%fused_computation | convolution fusion | flops 25769803776 | bytes 42991616 | tf_op jit(solution)/shard_map/aib,bc->aic/dot_general | solution.py:8
  270.2 7.2 %all-gather.11.cloned.1.call-done = f32[256,16,256]{2,0,1:T(8,128)} async-done(((f32[128,16,256]{2,0,1:T(8,128)}), f32[256,16,256]{2,0,1:T(8,128)}) %all-gather.11.cloned.1.call-update) | async-done | bytes 4194320 | tf_op jit(solution)/shard_map/all_gather | solution.py:15
  277.4 10.6 %fusion.12 = f32[512,256]{1,0:T(8,128)} fusion(f32[256,16,256]{2,0,1:T(8,128)} %all-gather.11.cloned.1.call-done, f32[256,512,16]{0,1,2:T(8,128)} %fusion), kind=kOutput, calls=%fused_computation.8 | convolution fusion | flops 6442450944 | bytes 13107200 | tf_op jit(solution)/shard_map/aic,sic->as/dot_general | solution.py:9
  288.0 0.0 all-reduce.5.cloned.1.call-update
  288.1 90.8 %all-reduce.5.cloned.1.call-done = f32[512,256]{1,0:T(8,128)} async-done(((f32[512,256]{1,0:T(8,128)}), f32[512,256]{1,0:T(8,128)}) %all-reduce.5.cloned.1.call-update) | async-done | bytes 524304 | tf_op jit(solution)/shard_map/psum | solution.py:23
  378.8 1.9 copy.23
Async XLA Ops:
  6.5 25.8 %all-gather.5.cloned.1.call-start = ((), (), s32[]{:S(2)}) async-start(), calls=%async_computation | async-start | bytes 1572864 | tf_op jit(solution)/shard_map/all_gather | solution.py:16
  7.3 83.4 %all-gather.7.cloned.1.call-start = ((), (), s32[]{:S(2)}) async-start(), calls=%async_computation.1 | async-start | bytes 6291456 | tf_op jit(solution)/shard_map/all_gather | solution.py:14
  8.0 188.6 %all-reduce.3.cloned.1.call-start = ((), (), s32[]{:S(2)}) async-start(), calls=%async_computation.2 | async-start | bytes 1048576 | tf_op jit(solution)/shard_map/psum | solution.py:23
  63.3 133.4 %copy-start = (f32[128,16,256]{2,1,0:T(8,128)S(1)}, f32[128,16,256]{2,1,0:T(8,128)}, u32[]{:S(2)}) copy-start(f32[128,16,256]{2,1,0:T(8,128)} %param.8) | copy-start | bytes 6291460
  105.8 113.5 %all-gather.9.cloned.1.call-start = ((), (), s32[]{:S(2)}) async-start(), calls=%async_computation.3 | async-start | bytes 1572864 | tf_op jit(solution)/shard_map/all_gather | solution.py:25
  196.7 80.8 %all-gather.11.cloned.1.call-start = ((), (), s32[]{:S(2)}) async-start(), calls=%async_computation.4 | async-start | bytes 6291456 | tf_op jit(solution)/shard_map/all_gather | solution.py:15
  199.3 179.6 %all-reduce.5.cloned.1.call-start = ((), (), s32[]{:S(2)}) async-start(), calls=%async_computation.5 | async-start | bytes 1048576 | tf_op jit(solution)/shard_map/psum | solution.py:23
Sparse Core Ops, SparseCore 0:
  8.9 23.3 all-gather.4
  33.9 56.7 all-gather.6
  105.9 90.6 all-reduce.2
  198.0 21.1 all-gather.8
  220.6 56.7 all-gather.10
  288.2 90.6 all-reduce.4
where the time goes:
time: 388 us
  waiting for transfers between devices  262 us (68%)
  matrix products  108 us (28%)
  between operations  13.5 us (3%)
  local copies, waits for them, and re-layouts  4.42 us (1%)
    psum x2, waiting for transfers between devices, shards(): summed = lax.psum(partial_sum, 'mode')  182 us
    dot_general x2, matrix products, chain_step(): jnp.einsum('aib,bc->aic', core, carried, precision=lax.Precision.HIGHEST)  81.9 us
    all_gather x1, waiting for transfers between devices, shards(): lax.all_gather(sketch_right, 'rank', axis=0, tiled=True)  27.4 us
    dot_general x2, matrix products, chain_step(): jnp.einsum('aic,sic->as', hidden, sketch, precision=lax.Precision.HIGHEST)  25.7 us
    all_gather x1, waiting for transfers between devices, shards(): lax.all_gather(carry_in, 'rank', axis=0, tiled=True)  24.3 us
    all_gather x1, waiting for transfers between devices, shards(): carried = lax.all_gather(summed, 'rank', axis=0, tiled=True)  19.7 us
  transfers between devices with their start and end apart: 6, of which 6 were waited for; matrix products, arithmetic and copies ran while one was open for 22% of the time, Pallas kernels for 0%

commit v1 on v0

--- a/solution.py
+++ b/solution.py
@@ -20,7 +20,7 @@
     result = carry_in
     for step in range(2):
         partial_sum = chain_step(cores[step], carried, sketches[step])
-        summed = lax.psum(partial_sum, "mode")
+        summed = jnp.sum(lax.all_gather(partial_sum, "mode"), axis=0)
         if step == 0:
             carried = lax.all_gather(summed, "rank", axis=0, tiled=True)
         else:

time: 388 us -> 360 us (0.928)
  waiting for transfers between devices: 262 us -> 223 us
  other arithmetic: 0 us -> 9.54 us
    psum x2 -> x0, waiting for transfers between devices: 182 us -> none  [shards(): summed = lax.psum(partial_sum, 'mode')]
    all_gather x0 -> x2, waiting for transfers between devices: none -> 151 us  [shards(): summed = jnp.sum(lax.all_gather(partial_sum, 'mode'), axis=0)]
    reduce_sum x0 -> x2, other arithmetic: none -> 9.54 us  [shards(): summed = jnp.sum(lax.all_gather(partial_sum, 'mode'), axis=0)]
  transfers between devices with their start and end apart: 6 -> 6, of which waited for: 6 -> 6; matrix products, arithmetic and copies ran while one was open for 22% -> 25% of each run, Pallas kernels for 0% -> 0%
where the time goes in v1:
time: 360 us; the launch traced here: 359 us
  waiting for transfers between devices  223 us (62%)
  matrix products  106 us (29%)
  between operations  13.5 us (4%)
  other arithmetic  9.54 us (3%)
  local copies, waits for them, and re-layouts  6.69 us (2%)
    all_gather x2, waiting for transfers between devices, shards(): summed = jnp.sum(lax.all_gather(partial_sum, 'mode'), axis=0)  151 us
    dot_general x2, matrix products, chain_step(): jnp.einsum('aib,bc->aic', core, carried, precision=lax.Precision.HIGHEST)  81.9 us
    all_gather x1, waiting for transfers between devices, shards(): lax.all_gather(sketch_right, 'rank', axis=0, tiled=True)  27.4 us
    dot_general x2, matrix products, chain_step(): jnp.einsum('aic,sic->as', hidden, sketch, precision=lax.Precision.HIGHEST)  23.7 us
    all_gather x1, waiting for transfers between devices, shards(): lax.all_gather(carry_in, 'rank', axis=0, tiled=True)  20.8 us
    all_gather x1, waiting for transfers between devices, shards(): carried = lax.all_gather(summed, 'rank', axis=0, tiled=True)  16.4 us
    reduce_sum x2, other arithmetic, shards(): summed = jnp.sum(lax.all_gather(partial_sum, 'mode'), axis=0)  9.54 us
    all_gather x1, waiting for transfers between devices, shards(): lax.all_gather(sketch_left, 'rank', axis=0, tiled=True)  7.2 us
  transfers between devices with their start and end apart: 6, of which 6 were waited for; matrix products, arithmetic and copies ran while one was open for 25% of the time, Pallas kernels for 0%

profile of v1, /device:TPU:1, one launch (start us, length us, event | category | flops | bytes accessed | tf_op | source)
XLA Modules:
  0.0 359.2 jit_solution(1580393514450074909)
XLA Ops:
  6.5 0.0 all-gather.9.cloned.1.call-start
  6.5 0.7 all-gather.9.cloned.1.call-update
  7.3 0.0 all-gather.11.cloned.1.call-start
  7.3 4.1 %copy.6 = f32[128,16,256]{2,0,1:T(8,128)} copy(f32[128,16,256]{2,1,0:T(8,128)} %param.6) | data formatting | bytes 4194304 | tf_op args[1]
  11.4 0.0 all-gather.11.cloned.1.call-update
  11.5 0.0 all-gather.17.cloned.1.call-start
  11.5 20.8 %all-gather.9.cloned.1.call-done = f32[1024,256]{1,0:T(8,128)} async-done(((f32[512,256]{1,0:T(8,128)}), f32[1024,256]{1,0:T(8,128)}) %all-gather.9.cloned.1.call-update) | async-done | bytes 1048592 | tf_op jit(solution)/shard_map/all_gather | solution.py:16
  32.3 31.0 %fusion.13 = f32[512,16,256]{2,1,0:T(8,128)} fusion(f32[512,16,1024]{2,1,0:T(8,128)} %param.5, f32[1024,256]{1,0:T(8,128)} %all-gather.9.cloned.1.call-done), kind=kOutput, calls=%fused_computation.9 | convolution fusion | flops 25769803776 | bytes 42991616 | tf_op jit(solution)/shard_map/aib,bc->aic/dot_general | solution.py:8
  63.3 27.4 %all-gather.11.cloned.1.call-done = f32[256,16,256]{2,0,1:T(8,128)} async-done(((f32[128,16,256]{2,0,1:T(8,128)}), f32[256,16,256]{2,0,1:T(8,128)}) %all-gather.11.cloned.1.call-update) | async-done | bytes 4194320 | tf_op jit(solution)/shard_map/all_gather | solution.py:14
  90.7 13.1 %fusion.6 = f32[512,256]{1,0:T(8,128)} fusion(f32[256,16,256]{2,0,1:T(8,128)} %all-gather.11.cloned.1.call-done, f32[512,16,256]{2,1,0:T(8,128)} %fusion.13), kind=kOutput, calls=%fused_computation.6 | convolution fusion | flops 6442450944 | bytes 13107200 | tf_op jit(solution)/shard_map/aic,sic->as/dot_general | solution.py:9
  103.8 0.0 copy-start
  103.8 0.0 all-gather.17.cloned.1.call-update
  103.8 0.0 all-gather.13.cloned.1.call-start
  103.8 75.4 %all-gather.17.cloned.1.call-done = f32[8192,256]{1,0:T(8,128)} async-done(((f32[512,256]{1,0:T(8,128)}), f32[8192,256]{1,0:T(8,128)}) %all-gather.17.cloned.1.call-update) | async-done | bytes 8388624 | tf_op jit(solution)/shard_map/all_gather | solution.py:23
  179.3 4.8 %reduce_sum.18 = f32[512,256]{1,0:T(8,128)} reduce(f32[16,512,256]{2,1,0:T(8,128)} %bitcast.20, f32[]{:T(128)} %constant.0.clone.1), dimensions={0}, to_apply=%region_0.0 | reduce | flops 1966080 | bytes 8912900 | tf_op jit(solution)/shard_map/reduce_sum | solution.py:23
  184.0 0.0 all-gather.13.cloned.1.call-update
  184.1 0.2 all-gather.15.cloned.1.call-start
  184.3 0.0 copy-done
  184.3 2.5 copy.7
  186.8 0.0 all-gather.15.cloned.1.call-update
  186.9 0.0 all-gather.19.cloned.1.call-start
  186.9 16.4 %all-gather.13.cloned.1.call-done = f32[1024,256]{1,0:T(8,128)} async-done(((f32[512,256]{1,0:T(8,128)}), f32[1024,256]{1,0:T(8,128)}) %all-gather.13.cloned.1.call-update) | async-done | bytes 1048592 | tf_op jit(solution)/shard_map/all_gather | solution.py:25
  203.3 51.0 %fusion = f32[256,512,16]{0,1,2:T(8,128)} fusion(f32[512,16,1024]{2,1,0:T(8,128)} %param.7, f32[1024,256]{1,0:T(8,128)} %all-gather.13.cloned.1.call-done), kind=kOutput, calls=%fused_computation | convolution fusion | flops 25769803776 | bytes 42991616 | tf_op jit(solution)/shard_map/aib,bc->aic/dot_general | solution.py:8
  254.3 7.2 %all-gather.15.cloned.1.call-done = f32[256,16,256]{2,0,1:T(8,128)} async-done(((f32[128,16,256]{2,0,1:T(8,128)}), f32[256,16,256]{2,0,1:T(8,128)}) %all-gather.15.cloned.1.call-update) | async-done | bytes 4194320 | tf_op jit(solution)/shard_map/all_gather | solution.py:15
  261.5 10.6 %fusion.9 = f32[512,256]{1,0:T(8,128)} fusion(f32[256,16,256]{2,0,1:T(8,128)} %all-gather.15.cloned.1.call-done, f32[256,512,16]{0,1,2:T(8,128)} %fusion), kind=kOutput, calls=%fused_computation.7 | convolution fusion | flops 6442450944 | bytes 13107200 | tf_op jit(solution)/shard_map/aic,sic->as/dot_general | solution.py:9
  272.1 0.0 all-gather.19.cloned.1.call-update
  272.1 75.5 %all-gather.19.cloned.1.call-done = f32[8192,256]{1,0:T(8,128)} async-done(((f32[512,256]{1,0:T(8,128)}), f32[8192,256]{1,0:T(8,128)}) %all-gather.19.cloned.1.call-update) | async-done | bytes 8388624 | tf_op jit(solution)/shard_map/all_gather | solution.py:23
  347.6 4.8 %reduce_sum.19 = f32[512,256]{1,0:T(8,128)} reduce(f32[16,512,256]{2,1,0:T(8,128)} %bitcast.21, f32[]{:T(128)} %constant.0.clone.1), dimensions={0}, to_apply=%region_1.0 | reduce | flops 1966080 | bytes 8912900 | tf_op jit(solution)/shard_map/reduce_sum | solution.py:23
Async XLA Ops:
  6.5 25.8 %all-gather.9.cloned.1.call-start = ((), (), s32[]{:S(2)}) async-start(), calls=%async_computation | async-start | bytes 1572864 | tf_op jit(solution)/shard_map/all_gather | solution.py:16
  7.3 83.4 %all-gather.11.cloned.1.call-start = ((), (), s32[]{:S(2)}) async-start(), calls=%async_computation.1 | async-start | bytes 6291456 | tf_op jit(solution)/shard_map/all_gather | solution.py:14
  11.5 167.8 %all-gather.17.cloned.1.call-start = ((), (), s32[]{:S(2)}) async-start(), calls=%async_computation.4 | async-start | bytes 8912896 | tf_op jit(solution)/shard_map/all_gather | solution.py:23
  103.8 80.5 %copy-start = (f32[128,16,256]{2,1,0:T(8,128)S(1)}, f32[128,16,256]{2,1,0:T(8,128)}, u32[]{:S(2)}) copy-start(f32[128,16,256]{2,1,0:T(8,128)} %param.8) | copy-start | bytes 6291460
  103.8 99.6 %all-gather.13.cloned.1.call-start = ((), (), s32[]{:S(2)}) async-start(), calls=%async_computation.2 | async-start | bytes 1572864 | tf_op jit(solution)/shard_map/all_gather | solution.py:25
  184.1 77.5 %all-gather.15.cloned.1.call-start = ((), (), s32[]{:S(2)}) async-start(), calls=%async_computation.3 | async-start | bytes 6291456 | tf_op jit(solution)/shard_map/all_gather | solution.py:15
  186.9 160.8 %all-gather.19.cloned.1.call-start = ((), (), s32[]{:S(2)}) async-start(), calls=%async_computation.5 | async-start | bytes 8912896 | tf_op jit(solution)/shard_map/all_gather | solution.py:23
Sparse Core Ops, SparseCore 0:
  8.9 23.3 all-gather.8
  33.9 56.7 all-gather.10
  103.9 75.3 all-gather.16
  184.2 19.1 all-gather.12
  204.7 56.7 all-gather.14
  272.3 75.3 all-gather.18
